TPU v7x, 128 devices: a whole 4x4x4 slice. The times are simulated.
128 devices in a mesh: gx: 8 (over y, core), gy: 16 (over x, z).
Axes of the slice: x: 4, y: 4, z: 4, core: 2. Of those that a mesh axis runs over, the one named last changes fastest.
Arguments:
- cell_state: float32 [16, 1048576], P(None, ('gx', 'gy')), may hold values from -6 to 6
- geometry: float32 [7, 524288], P(None, ('gx', 'gy')), may hold values from -8 to 8, as said below
- surface_cell: int32 [524288], P(('gx', 'gy')), may hold values from 0 to 8191
- counts: int32 [128], P(('gx', 'gy')), may hold values from 128 to 4096, as said below
- wavenumbers: float32 [4], replicated, may hold values from 8 to 24
- target: float32 [4, 2, 2048], replicated, may hold values from -6 to 6
- direction_weight: float32 [2048], replicated, may hold values from 0.3 to 3
Outputs:
- far_field: float32 [4, 2, 2048], replicated
- objective: float32 [], replicated
- cell_adjoint: float32 [16, 1048576], P(None, ('gx', 'gy'))
Inputs may be any that keep to these rules, and one draw needn't show every extreme that they name: Every count is a multiple of 128; one device's count is 4096; all counts together make 128 * 1024. `geometry`: rows 3 to 5 are unit vectors; row 6 is positive.
All inputs are finite; a program needn't handle non-finite values.
Results may differ from a plain program's by a relative error of at most 0.022.
Values sent between devices are 32-bit elements; how exact they have to be, the bound alone decides.
A program may use at most 128 MiB of HBM per device.

v0:
```python
import math
import jax
import jax.numpy as jnp
from jax import lax
from jax.sharding import PartitionSpec as P

GOLDEN = math.pi * (3.0 - math.sqrt(5.0))


def directions(count_dirs):
    lattice = jnp.arange(count_dirs).astype(jnp.float32)
    height = 1.0 - (2.0 * lattice + 1.0) / count_dirs
    radius_xy = jnp.sqrt(1.0 - height * height)
    azimuth = jnp.mod(lattice * GOLDEN, 2.0 * math.pi)
    return (radius_xy * jnp.cos(azimuth), radius_xy * jnp.sin(azimuth), height)


def kernel_block(points, wavenum, east_x, north_y, upward):
    phases = wavenum * (
        points[0][:, None] * east_x[None, :]
        + points[1][:, None] * north_y[None, :]
        + points[2][:, None] * upward[None, :]
    )
    return jnp.concatenate([jnp.cos(phases), jnp.sin(phases)], axis=1).astype(jnp.bfloat16)


def source_rows(rows_block, level):
    surface_area = rows_block[22]
    normal = rows_block[19:22]
    pressure_real = rows_block[level] * surface_area
    pressure_imag = rows_block[4 + level] * surface_area
    return jnp.stack(
        [
            rows_block[8 + level] * surface_area,
            normal[0] * pressure_real,
            normal[1] * pressure_real,
            normal[2] * pressure_real,
            rows_block[12 + level] * surface_area,
            normal[0] * pressure_imag,
            normal[1] * pressure_imag,
            normal[2] * pressure_imag,
        ]
    ).astype(jnp.bfloat16)


def far_field_of(sums, wavenumbers, direction_basis):
    half_width = sums.shape[2] // 2
    cosine_part = sums[:, :, :half_width]
    sine_part = sums[:, :, half_width:]
    real_q = cosine_part[:, 0:4] + sine_part[:, 4:8]
    imag_q = cosine_part[:, 4:8] - sine_part[:, 0:4]
    real_z = jnp.sum(direction_basis[None] * real_q, axis=1)
    imag_z = jnp.sum(direction_basis[None] * imag_q, axis=1)
    wavenum = wavenumbers[:, None]
    return jnp.stack([-wavenum * imag_z, wavenum * real_z], axis=1)


def adjoint_weights(far_field, target, direction_weight, wavenumbers, direction_basis):
    count_dirs = far_field.shape[2]
    mismatch = far_field - target
    objective = jnp.sum(direction_weight * mismatch * mismatch) / count_dirs
    gradient = 2.0 * direction_weight * mismatch / count_dirs
    wavenum = wavenumbers[:, None]
    real_gz = wavenum * gradient[:, 1]
    imag_gz = -wavenum * gradient[:, 0]
    real_gq = direction_basis[None] * real_gz[:, None]
    imag_gq = direction_basis[None] * imag_gz[:, None]
    upper_half = jnp.concatenate([real_gq, -imag_gq], axis=2)
    lower_half = jnp.concatenate([imag_gq, real_gq], axis=2)
    return (objective, jnp.concatenate([upper_half, lower_half], axis=1).astype(jnp.bfloat16))


def adjoint_sources(products, normal):
    pressure_real = jnp.sum(normal[None] * products[:, 1:4], axis=1)
    pressure_imag = jnp.sum(normal[None] * products[:, 5:8], axis=1)
    return jnp.concatenate([pressure_real, pressure_imag, products[:, 0], products[:, 4]], axis=0)


def on_device(cell_state, geometry, surface_cell, counts, wavenumbers, target, direction_weight):
    owners = lax.axis_size(("gx", "gy"))
    rows_dev = surface_cell.shape[0]
    capacity = rows_dev // owners
    live_own = rows_dev // 4
    count_dirs = target.shape[2]
    num_freqs = wavenumbers.shape[0]
    living = (jnp.arange(rows_dev) < counts[0]).astype(jnp.float32)
    outgoing = (
        jnp.concatenate(
            [cell_state[:, surface_cell], geometry, jnp.ones((1, rows_dev), jnp.float32)], axis=0
        )
        * living[None, :]
    )
    outgoing = outgoing.reshape(24, capacity, owners)
    arrived = lax.all_to_all(outgoing, ("gx", "gy"), split_axis=2, concat_axis=2, tiled=True)
    marker = arrived[23]
    per_source = jnp.sum(marker, axis=0).astype(jnp.int32)
    offset = jnp.cumsum(per_source) - per_source
    position = offset[None, :] + jnp.arange(capacity, dtype=jnp.int32)[:, None]
    packed_slot = jnp.where(marker > 0.5, position, live_own).reshape(capacity * owners)
    compact = (
        jnp.zeros((23, live_own), jnp.float32)
        .at[:, packed_slot]
        .set(arrived[:23].reshape(23, capacity * owners), mode="drop")
    )
    block_rows = math.gcd(live_own, 1024)
    block_count = live_own // block_rows
    blocks = compact.reshape(23, block_count, block_rows).transpose(1, 0, 2)
    east_x, north_y, upward = directions(count_dirs)
    direction_basis = jnp.stack([jnp.ones_like(east_x), east_x, north_y, upward])

    def forward_block(running, rows_block):
        products = [
            jnp.dot(
                source_rows(rows_block, level),
                kernel_block(rows_block[16:19], wavenumbers[level], east_x, north_y, upward),
                preferred_element_type=jnp.float32,
            )
            for level in range(num_freqs)
        ]
        return (running + jnp.stack(products), None)

    sums, _ = lax.scan(
        forward_block, jnp.zeros((num_freqs, 8, 2 * count_dirs), jnp.float32), blocks
    )
    far_field = lax.psum(far_field_of(sums, wavenumbers, direction_basis), ("gx", "gy"))
    objective, weights = adjoint_weights(
        far_field, target, direction_weight, wavenumbers, direction_basis
    )

    def adjoint_block(carry, rows_block):
        products = [
            lax.dot_general(
                weights[level],
                kernel_block(rows_block[16:19], wavenumbers[level], east_x, north_y, upward),
                (((1,), (1,)), ((), ())),
                preferred_element_type=jnp.float32,
            )
            for level in range(num_freqs)
        ]
        return (carry, adjoint_sources(jnp.stack(products), rows_block[19:22]))

    _, backward = lax.scan(adjoint_block, jnp.zeros((), jnp.float32), blocks)
    backward = backward.transpose(1, 0, 2).reshape(16, live_own)
    spread = backward[:, jnp.minimum(packed_slot, live_own - 1)] * marker.reshape(
        1, capacity * owners
    )
    spread = spread.reshape(16, capacity, owners)
    returned = lax.all_to_all(spread, ("gx", "gy"), split_axis=2, concat_axis=2, tiled=True)
    per_row = returned.reshape(16, rows_dev) * living[None, :]
    cell_adjoint = jnp.zeros(cell_state.shape, jnp.float32).at[:, surface_cell].add(per_row)
    return (far_field, objective, cell_adjoint)


def solution(mesh):
    placed = (
        P(None, ("gx", "gy")),
        P(None, ("gx", "gy")),
        P(("gx", "gy")),
        P(("gx", "gy")),
        P(),
        P(),
        P(),
    )
    return jax.shard_map(
        on_device,
        mesh=mesh,
        in_specs=placed,
        out_specs=(P(), P(), P(None, ("gx", "gy"))),
        check_vma=False,
    )
```

profile of v0, /device:TPU:1, one launch (start us, length us, event | category | flops | bytes accessed | tf_op | source)
XLA Modules:
  0.0 461.3 jit_solution(930296876396630908)
XLA Ops:
  10.5 3.5 copy.346
  14.0 12.9 %gather_fusion = f32[4096,16]{1,0:T(8,128)S(1)} fusion(f32[16,8192]{0,1:T(8,128)} %copy.346, s32[4096]{0:T(1024)S(1)} %get-tuple-element.118), kind=kCustom, calls=%fused_computation | custom fusion | bytes 540672 | tf_op jit(solution)/shard_map/gather | solution.py:89
  28.1 1.3 fusion.51
  29.4 1.4 reshape.322
  30.8 11.5 %all-to-all-start = ((f32[128,1,768]{2,1,0:T(1,128)}), f32[128,1,768]{2,1,0:T(1,128)S(1)}, u32[]{:S(2)}, u32[]{:S(2)}) async-start(f32[128,1,768]{2,1,0:T(1,128)} %reshape.322), calls=%async_computation | async-start | bytes 786432 | tf_op jit(solution)/shard_map/all_to_all | solution.py:94
  43.5 11.0 %all-to-all-done = f32[128,1,768]{2,1,0:T(1,128)S(1)} async-done(((f32[128,1,768]{2,1,0:T(1,128)}), f32[128,1,768]{2,1,0:T(1,128)S(1)}, u32[]{:S(2)}, u32[]{:S(2)}) %all-to-all-start) | async-done | bytes 393248 | tf_op jit(solution)/shard_map/all_to_all | solution.py:94
  55.0 1.5 reduce.8
  59.9 11.2 %scatter_custom_fusion = f32[23,1024]{0,1:T(8,128)S(1)} fusion(s32[4096]{0:T(1024)S(1)} %bitcast.117, f32[4096,23]{1,0:T(8,128)S(1)} %copy.352, f32[]{:T(128)} %constant.23.clone.1), kind=kCustom, calls=%fused_computation.48 | custom fusion | bytes 94212 | tf_op jit(solution)/shard_map/scatter | solution.py:103
  71.1 1.4 slice_reduce_fusion.2
  72.6 5.4 %fusion.49 = (f32[1,1024]{0,1:T(8,128)}, f32[1,1024]{0,1:T(8,128)}, f32[1,1024]{0,1:T(8,128)}, f32[1,1024]{0,1:T(8,128)}, f32[1,1024]{0,1:T(8,128)}, /*index=5*/...) fusion(f32[23,1024]{0,1:T(8,128)S(1)} %scatter_custom_fusion), kind=kLoop, calls=%fused_computation.158 | loop fusion | bytes 155648 | tf_op jit(solution)/shard_map/while/body/eval_jaxpr/slice | solution.py:31
  81.7 1.2 copy.401
  82.9 1.2 copy.400
  84.2 1.2 copy.399
  89.1 1.2 copy.395
  90.3 1.2 copy.394
  91.6 1.2 copy.393
  97.7 126.3 %cosine_convert_fusion.3 = (bf16[1024,2048]{1,0:T(8,128)(2,1)S(1)}, bf16[1024,2048]{1,0:T(8,128)(2,1)}, bf16[1024,2048]{1,0:T(8,128)(2,1)}, bf16[1024,2048]{1,0:...) fusion(f32[2048]{0:T(1024)S(1)} %multiply_subtract_fusion, ...), kind=kLoop, calls=%fused_computation.15 | loop fusion | flops 35651584 | bytes 33591312 | tf_op jit(solution)/shard_map/convert.36
  226.0 1.3 copy-done.2
  227.4 4.1 fusion.14
  231.6 4.1 fusion.13
  235.8 4.3 fusion.15
  241.6 133.9 %all-reduce.2.cloned.1.call-done = f32[4,2,2048]{2,0,1:T(4,128)} async-done(((f32[4,2,2048]{2,0,1:T(4,128)}), f32[4,2,2048]{2,0,1:T(4,128)}) %all-reduce.2.cloned.1.call-update) | async-done | bytes 65552 | tf_op jit(solution)/shard_map/psum | solution.py:125
  375.5 1.5 multiply_multiply_fusion.1
  377.3 4.8 %fusion.21 = f32[1,8,1024]{2,1,0:T(8,128)S(1)} fusion(bf16[1024,2048]{1,0:T(8,128)(2,1)} %get-tuple-element.112, bf16[1024,2048]{1,0:T(8,128)(2,1)} %get-tuple-element.113, bf16[4,8,4096]{2,1,0:T(8,128)(2,1)S(1)} %maximum_maximum_fusion), kind=kOutput, calls=%fused_computation.39 | convolution fusion | flops 83886080 | bytes 8486912 | tf_op jit(solution)/shard_map/while/body/eval_jaxpr/dot_general | solution.py:132
  383.2 2.3 fusion.20
  386.7 2.3 fusion.19
  390.2 2.3 fusion.18
  392.9 10.8 %gather_fusion.1 = f32[4096,16]{1,0:T(8,128)S(1)} fusion(f32[16,1024]{0,1:T(8,128)S(1)} %copy.376, s32[4096]{0:T(1024)S(1)} %broadcast_clamp_fusion), kind=kCustom, calls=%fused_computation.1 | custom fusion | bytes 540672 | tf_op jit(solution)/shard_map/gather | solution.py:144
  406.0 5.4 %all-to-all-start.1 = ((f32[128,1,512]{2,1,0:T(1,128)}), f32[128,1,512]{2,1,0:T(1,128)S(1)}, u32[]{:S(2)}, u32[]{:S(2)}) async-start(f32[128,1,512]{2,1,0:T(1,128)} %reshape.324), calls=%async_computation.1 | async-start | bytes 524288 | tf_op jit(solution)/shard_map/all_to_all | solution.py:148
  412.8 9.7 %all-to-all-done.1 = f32[128,1,512]{2,1,0:T(1,128)S(1)} async-done(((f32[128,1,512]{2,1,0:T(1,128)}), f32[128,1,512]{2,1,0:T(1,128)S(1)}, u32[]{:S(2)}, u32[]{:S(2)}) %all-to-all-start.1) | async-done | bytes 262176 | tf_op jit(solution)/shard_map/all_to_all | solution.py:148
  425.1 24.5 %scatter_custom_fusion.1 = f32[16,8192]{0,1:T(8,128)} fusion(s32[4096]{0:T(1024)S(1)} %get-tuple-element.117, f32[4096,16]{1,0:T(8,128)S(1)} %copy.380, f32[]{:T(128)} %constant.23.clone.1), kind=kCustom, calls=%fused_computation.33 | custom fusion | flops 65536 | bytes 524292 | tf_op jit(solution)/shard_map/scatter-add | solution.py:150
  449.6 3.5 copy.382
  (105 shorter events, 34.5 us)
Async XLA Ops:
  26.9 15.8 %copy-start.11 = (f32[4]{0:T(128)S(1)}, f32[4]{0:T(128)}, u32[]{:S(2)}) copy-start(f32[4]{0:T(128)} %param.11) | copy-start | bytes 52
  26.9 16.4 %copy-start.10 = (f32[2048]{0:T(1024)S(1)}, f32[2048]{0:T(1024)}, u32[]{:S(2)}) copy-start(f32[2048]{0:T(1024)} %param.13) | copy-start | bytes 24580
  30.8 23.6 %all-to-all-start = ((f32[128,1,768]{2,1,0:T(1,128)}), f32[128,1,768]{2,1,0:T(1,128)S(1)}, u32[]{:S(2)}, u32[]{:S(2)}) async-start(f32[128,1,768]{2,1,0:T(1,128)} %reshape.322), calls=%async_computation | async-start | bytes 786432 | tf_op jit(solution)/shard_map/all_to_all | solution.py:94
  42.3 333.1 %all-reduce.2.cloned.1.call-start = ((), (), s32[]{:S(2)}) async-start(), calls=%async_computation.2 | async-start | bytes 131072 | tf_op jit(solution)/shard_map/psum | solution.py:125
  224.0 1.9 copy-start
  224.0 3.3 copy-start.2
  235.8 139.7 %copy-start.9 = (f32[4,2,2048]{2,1,0:T(2,128)S(1)}, f32[4,2,2048]{2,1,0:T(2,128)}, u32[]{:S(2)}) copy-start(f32[4,2,2048]{2,1,0:T(2,128)} %param.12) | copy-start | bytes 196612
  377.3 4.8 %copy-start.6 = (bf16[1024,2048]{1,0:T(8,128)(2,1)S(1)}, bf16[1024,2048]{1,0:T(8,128)(2,1)}, u32[]{:S(2)}) copy-start(bf16[1024,2048]{1,0:T(8,128)(2,1)} %get-tuple-element.107) | copy-start | bytes 12582916
  377.3 5.9 %copy-start.7 = (bf16[1024,2048]{1,0:T(8,128)(2,1)S(1)}, bf16[1024,2048]{1,0:T(8,128)(2,1)}, u32[]{:S(2)}) copy-start(bf16[1024,2048]{1,0:T(8,128)(2,1)} %get-tuple-element.111) | copy-start | bytes 12582916
  383.2 2.3 copy-start.4
  383.2 3.5 copy-start.5
  386.7 2.3 copy-start.1
  386.7 3.5 copy-start.3
  392.8 19.2 %copy-start.8 = (f32[4,2,2048]{2,0,1:T(4,128)S(1)}, f32[4,2,2048]{2,0,1:T(4,128)}, u32[]{:S(2)}) copy-start(f32[4,2,2048]{2,0,1:T(4,128)} %all-reduce.2.cloned.1.call-done) | copy-start | bytes 196612
  406.0 16.5 %all-to-all-start.1 = ((f32[128,1,512]{2,1,0:T(1,128)}), f32[128,1,512]{2,1,0:T(1,128)S(1)}, u32[]{:S(2)}, u32[]{:S(2)}) async-start(f32[128,1,512]{2,1,0:T(1,128)} %reshape.324), calls=%async_computation.1 | async-start | bytes 524288 | tf_op jit(solution)/shard_map/all_to_all | solution.py:148
Sparse Core Ops, SparseCore 0:
  241.3 134.1 all-reduce.1
where the time goes:
time: 469 us; the launch traced here: 461 us
  other arithmetic  161 us (34%)
  waiting for transfers between devices  155 us (33%)
  local copies, waits for them, and re-layouts  86.5 us (18%)
  matrix products  25.3 us (5%)
  between operations  17.1 us (4%)
  starting transfers between devices  17 us (4%)
    psum x1, waiting for transfers between devices, on_device(): lax.psum(far_field_of(sums, wavenumbers, direction_basis), ('gx', 'gy'))  134 us
    another operation x6, other arithmetic  127 us
    unnamed x57, local copies, waits for them, and re-layouts  37.4 us
    scatter-add x1, other arithmetic, on_device(): jnp.zeros(cell_state.shape, jnp.float32).at[:, surface_cell].add(per_row)  24.5 us
    dot_general x4, matrix products, forward_block(): jnp.dot(source_rows(rows_block, level), kernel_block(rows_block[16:19], w...  13.8 us
    gather x1, local copies, waits for them, and re-layouts, on_device(): cell_state[:, surface_cell]  12.9 us
    gather x2, local copies, waits for them, and re-layouts, on_device(): backward[:, jnp.minimum(packed_slot, live_own - 1)]  11.8 us
    dot_general x4, matrix products, adjoint_block(): lax.dot_general(weights[level], kernel_block(rows_block[16:19], wavenumbe...  11.6 us
  transfers between devices with their start and end apart: 3, of which 3 were waited for; matrix products, arithmetic and copies ran while one was open for 0% of the time, Pallas kernels for 0%

commit v1 on v0

--- a/solution.py
+++ b/solution.py
@@ -122,7 +122,9 @@
     sums, _ = lax.scan(
         forward_block, jnp.zeros((num_freqs, 8, 2 * count_dirs), jnp.float32), blocks
     )
-    far_field = lax.psum(far_field_of(sums, wavenumbers, direction_basis), ("gx", "gy"))
+    far_field = jnp.sum(
+        lax.all_gather(far_field_of(sums, wavenumbers, direction_basis), ("gx", "gy")), axis=0
+    )
     objective, weights = adjoint_weights(
         far_field, target, direction_weight, wavenumbers, direction_basis
     )

time: 469 us -> 415 us (0.88)
  waiting for transfers between devices: 155 us -> 87.8 us
  local copies, waits for them, and re-layouts: 86.5 us -> 93.5 us
  other arithmetic: 161 us -> 166 us
    psum x1 -> x0, waiting for transfers between devices: 134 us -> none  [on_device(): lax.psum(far_field_of(sums, wavenumbers, direction_basis), ('gx', 'gy'))]
    all_gather x0 -> x1, waiting for transfers between devices: none -> 66.6 us  [on_device(): lax.all_gather(far_field_of(sums, wavenumbers, direction_basis), ('gx', '...]
    reduce_sum x0 -> x1, other arithmetic: none -> 6.91 us  [on_device(): jnp.sum(lax.all_gather(far_field_of(sums, wavenumbers, direction_basis),...]
    gather x2, local copies, waits for them, and re-layouts: 11.8 us -> 16.8 us  [on_device(): backward[:, jnp.minimum(packed_slot, live_own - 1)]]
    unnamed x57 -> x58, local copies, waits for them, and re-layouts: 37.4 us -> 35.6 us
where the time goes in v1:
time: 415 us; the launch traced here: 407 us
  other arithmetic  166 us (40%)
  local copies, waits for them, and re-layouts  93.5 us (23%)
  waiting for transfers between devices  87.8 us (21%)
  matrix products  25.7 us (6%)
  between operations  17.3 us (4%)
  starting transfers between devices  16.9 us (4%)
    another operation x6, other arithmetic  127 us
    all_gather x1, waiting for transfers between devices, on_device(): lax.all_gather(far_field_of(sums, wavenumbers, direction_basis), ('gx', '...  66.6 us
    unnamed x58, local copies, waits for them, and re-layouts  35.6 us
    scatter-add x1, other arithmetic, on_device(): jnp.zeros(cell_state.shape, jnp.float32).at[:, surface_cell].add(per_row)  24.5 us
    gather x2, local copies, waits for them, and re-layouts, on_device(): backward[:, jnp.minimum(packed_slot, live_own - 1)]  16.8 us
    gather x1, local copies, waits for them, and re-layouts, on_device(): cell_state[:, surface_cell]  16.3 us
    dot_general x4, matrix products, forward_block(): jnp.dot(source_rows(rows_block, level), kernel_block(rows_block[16:19], w...  13.8 us
    dot_general x4, matrix products, adjoint_block(): lax.dot_general(weights[level], kernel_block(rows_block[16:19], wavenumbe...  12 us
  transfers between devices with their start and end apart: 3, of which 3 were waited for; matrix products, arithmetic and copies ran while one was open for 0% of the time, Pallas kernels for 0%

profile of v1, /device:TPU:1, one launch (start us, length us, event | category | flops | bytes accessed | tf_op | source)
XLA Modules:
  0.0 407.3 jit_solution(16268694652465154338)
XLA Ops:
  9.7 3.5 copy.348
  13.2 16.3 %gather_fusion = f32[4096,16]{1,0:T(8,128)} fusion(f32[16,8192]{0,1:T(8,128)} %copy.348, s32[4096]{0:T(1024)S(1)} %get-tuple-element.118), kind=kCustom, calls=%fused_computation | custom fusion | bytes 540672 | tf_op jit(solution)/shard_map/gather | solution.py:89
  29.5 2.5 copy.349
  32.3 1.4 reshape.323
  33.8 11.5 %all-to-all-start = ((f32[128,1,768]{2,1,0:T(1,128)}), f32[128,1,768]{2,1,0:T(1,128)S(1)}, u32[]{:S(2)}, u32[]{:S(2)}) async-start(f32[128,1,768]{2,1,0:T(1,128)} %reshape.323), calls=%async_computation | async-start | bytes 786432 | tf_op jit(solution)/shard_map/all_to_all | solution.py:94
  46.5 10.9 %all-to-all-done = f32[128,1,768]{2,1,0:T(1,128)S(1)} async-done(((f32[128,1,768]{2,1,0:T(1,128)}), f32[128,1,768]{2,1,0:T(1,128)S(1)}, u32[]{:S(2)}, u32[]{:S(2)}) %all-to-all-start) | async-done | bytes 393248 | tf_op jit(solution)/shard_map/all_to_all | solution.py:94
  57.9 1.5 reduce.8
  62.8 10.9 %scatter_custom_fusion = f32[23,1024]{0,1:T(8,128)S(1)} fusion(s32[4096]{0:T(1024)S(1)} %bitcast.123, f32[4096,23]{1,0:T(8,128)S(1)} %copy.354, f32[]{:T(128)} %constant.23.clone.1), kind=kCustom, calls=%fused_computation.48 | custom fusion | bytes 94212 | tf_op jit(solution)/shard_map/scatter | solution.py:103
  73.8 1.4 slice_reduce_fusion.2
  75.2 5.4 %fusion.47 = (f32[1,1024]{0,1:T(8,128)}, f32[1,1024]{0,1:T(8,128)}, f32[1,1024]{0,1:T(8,128)}, f32[1,1024]{0,1:T(8,128)}, f32[1,1024]{0,1:T(8,128)}, /*index=5*/...) fusion(f32[23,1024]{0,1:T(8,128)S(1)} %scatter_custom_fusion), kind=kLoop, calls=%fused_computation.157 | loop fusion | bytes 155648 | tf_op jit(solution)/shard_map/while/body/eval_jaxpr/slice | solution.py:31
  85.6 1.2 copy.404
  86.8 1.2 copy.403
  88.0 1.2 copy.402
  89.3 1.2 copy.401
  94.2 1.2 copy.397
  100.4 126.4 %cosine_convert_fusion.3 = (bf16[1024,2048]{1,0:T(8,128)(2,1)S(1)}, bf16[1024,2048]{1,0:T(8,128)(2,1)}, bf16[1024,2048]{1,0:T(8,128)(2,1)}, bf16[1024,2048]{1,0:...) fusion(f32[2048]{0:T(1024)S(1)} %multiply_subtract_fusion, ...), kind=kLoop, calls=%fused_computation.15 | loop fusion | flops 35651584 | bytes 33591312 | tf_op jit(solution)/shard_map/convert.36
  226.7 1.9 copy-done
  230.1 4.1 %fusion.14 = f32[1,8,4096]{2,1,0:T(8,128)S(1)} fusion(bf16[8,1024]{1,0:T(8,128)(2,1)S(1)} %stack.140, bf16[1024,2048]{1,0:T(8,128)(2,1)} %get-tuple-element.111, bf16[1024,2048]{1,0:T(8,128)(2,1)} %get-tuple-element.107), kind=kOutput, calls=%fused_computation.31 | convolution fusion | flops 83886080 | bytes 8536064 | tf_op jit(solution)/shard_map/while/body/eval_jaxpr/dot_general | solution.py:113
  234.3 4.1 %fusion.13 = f32[1,8,4096]{2,1,0:T(8,128)S(1)} fusion(bf16[8,1024]{1,0:T(8,128)(2,1)S(1)} %stack.138, bf16[1024,2048]{1,0:T(8,128)(2,1)} %get-tuple-element.110, bf16[1024,2048]{1,0:T(8,128)(2,1)} %get-tuple-element.108), kind=kOutput, calls=%fused_computation.30 | convolution fusion | flops 83886080 | bytes 8536064 | tf_op jit(solution)/shard_map/while/body/eval_jaxpr/dot_general | solution.py:113
  238.5 4.3 %fusion.15 = f32[1,8,4096]{2,1,0:T(8,128)S(1)} fusion(bf16[8,1024]{1,0:T(8,128)(2,1)S(1)} %stack.142, bf16[1024,2048]{1,0:T(8,128)(2,1)} %get-tuple-element.112, bf16[1024,2048]{1,0:T(8,128)(2,1)} %get-tuple-element.113), kind=kOutput, calls=%fused_computation.32 | convolution fusion | flops 83886080 | bytes 8536064 | tf_op jit(solution)/shard_map/while/body/eval_jaxpr/dot_general | solution.py:113
  244.4 66.6 %all-gather.3.cloned.1.call-done = f32[512,2,2048]{2,1,0:T(2,128)} async-done(((f32[4,2,2048]{2,1,0:T(2,128)}), f32[512,2,2048]{2,1,0:T(2,128)}) %all-gather.3.cloned.1.call-update) | async-done | bytes 8388624 | tf_op jit(solution)/shard_map/all_gather | solution.py:126
  311.1 6.9 %reduce_sum.74 = f32[4,2,2048]{2,1,0:T(2,128)S(1)} reduce(f32[128,4,2,2048]{3,2,1,0:T(2,128)} %bitcast.103, f32[]{:T(128)} %constant.23.clone.1), dimensions={0}, to_apply=%region_5.6 | reduce | flops 2080768 | bytes 8454148 | tf_op jit(solution)/shard_map/reduce_sum | solution.py:125
  319.1 5.2 %fusion.21 = f32[1,8,1024]{2,1,0:T(8,128)S(1)} fusion(bf16[1024,2048]{1,0:T(8,128)(2,1)} %get-tuple-element.112, bf16[1024,2048]{1,0:T(8,128)(2,1)} %get-tuple-element.113, bf16[4,8,4096]{2,1,0:T(8,128)(2,1)S(1)} %maximum_maximum_fusion), kind=kOutput, calls=%fused_computation.39 | convolution fusion | flops 83886080 | bytes 8486912 | tf_op jit(solution)/shard_map/while/body/eval_jaxpr/dot_general | solution.py:134
  324.3 2.3 fusion.20
  327.8 2.3 fusion.19
  331.2 2.3 fusion.18
  333.9 14.3 %gather_fusion.1 = f32[4096,16]{1,0:T(8,128)} fusion(f32[16,1024]{0,1:T(8,128)S(1)} %copy.379, s32[4096]{0:T(1024)S(1)} %broadcast_clamp_fusion), kind=kCustom, calls=%fused_computation.1 | custom fusion | bytes 540672 | tf_op jit(solution)/shard_map/gather | solution.py:146
  348.2 2.5 copy.381
  352.0 5.3 %all-to-all-start.1 = ((f32[128,1,512]{2,1,0:T(1,128)}), f32[128,1,512]{2,1,0:T(1,128)S(1)}, u32[]{:S(2)}, u32[]{:S(2)}) async-start(f32[128,1,512]{2,1,0:T(1,128)} %reshape.325), calls=%async_computation.1 | async-start | bytes 524288 | tf_op jit(solution)/shard_map/all_to_all | solution.py:150
  358.0 10.2 %all-to-all-done.1 = f32[128,1,512]{2,1,0:T(1,128)S(1)} async-done(((f32[128,1,512]{2,1,0:T(1,128)}), f32[128,1,512]{2,1,0:T(1,128)S(1)}, u32[]{:S(2)}, u32[]{:S(2)}) %all-to-all-start.1) | async-done | bytes 262176 | tf_op jit(solution)/shard_map/all_to_all | solution.py:150
  370.8 24.5 %scatter_custom_fusion.1 = f32[16,8192]{0,1:T(8,128)} fusion(s32[4096]{0:T(1024)S(1)} %get-tuple-element.117, f32[4096,16]{1,0:T(8,128)S(1)} %copy.383, f32[]{:T(128)} %constant.23.clone.1), kind=kCustom, calls=%fused_computation.33 | custom fusion | flops 65536 | bytes 524292 | tf_op jit(solution)/shard_map/scatter-add | solution.py:152
  395.3 3.5 copy.384
  (107 shorter events, 31.6 us)
Async XLA Ops:
  9.5 36.2 %copy-start.11 = (f32[4]{0:T(128)S(1)}, f32[4]{0:T(128)}, u32[]{:S(2)}) copy-start(f32[4]{0:T(128)} %param.11) | copy-start | bytes 52
  33.8 23.6 %all-to-all-start = ((f32[128,1,768]{2,1,0:T(1,128)}), f32[128,1,768]{2,1,0:T(1,128)S(1)}, u32[]{:S(2)}, u32[]{:S(2)}) async-start(f32[128,1,768]{2,1,0:T(1,128)} %reshape.323), calls=%async_computation | async-start | bytes 786432 | tf_op jit(solution)/shard_map/all_to_all | solution.py:94
  45.3 265.8 %all-gather.3.cloned.1.call-start = ((), (), s32[]{:S(2)}) async-start(), calls=%async_computation.2 | async-start | bytes 8454144 | tf_op jit(solution)/shard_map/all_gather | solution.py:126
  226.7 1.9 copy-start
  226.7 3.3 copy-start.2
  238.4 5.6 %copy-start.10 = (f32[2048]{0:T(1024)S(1)}, f32[2048]{0:T(1024)}, u32[]{:S(2)}) copy-start(f32[2048]{0:T(1024)} %param.13) | copy-start | bytes 24580
  242.8 75.2 %copy-start.9 = (f32[4,2,2048]{2,1,0:T(2,128)S(1)}, f32[4,2,2048]{2,1,0:T(2,128)}, u32[]{:S(2)}) copy-start(f32[4,2,2048]{2,1,0:T(2,128)} %param.12) | copy-start | bytes 196612
  318.0 8.6 %copy-start.8 = (f32[4,2,2048]{2,1,0:T(2,128)}, f32[4,2,2048]{2,1,0:T(2,128)S(1)}, u32[]{:S(2)}) copy-start(f32[4,2,2048]{2,1,0:T(2,128)S(1)} %reduce_sum.74) | copy-start | bytes 196612
  318.0 6.3 %copy-start.6 = (bf16[1024,2048]{1,0:T(8,128)(2,1)S(1)}, bf16[1024,2048]{1,0:T(8,128)(2,1)}, u32[]{:S(2)}) copy-start(bf16[1024,2048]{1,0:T(8,128)(2,1)} %get-tuple-element.107) | copy-start | bytes 12582916
  318.0 6.3 %copy-start.7 = (bf16[1024,2048]{1,0:T(8,128)(2,1)S(1)}, bf16[1024,2048]{1,0:T(8,128)(2,1)}, u32[]{:S(2)}) copy-start(bf16[1024,2048]{1,0:T(8,128)(2,1)} %get-tuple-element.111) | copy-start | bytes 12582916
  324.3 2.3 copy-start.4
  324.3 3.5 copy-start.5
  327.8 2.3 copy-start.1
  327.8 3.5 copy-start.3
  352.0 16.2 %all-to-all-start.1 = ((f32[128,1,512]{2,1,0:T(1,128)}), f32[128,1,512]{2,1,0:T(1,128)S(1)}, u32[]{:S(2)}, u32[]{:S(2)}) async-start(f32[128,1,512]{2,1,0:T(1,128)} %reshape.325), calls=%async_computation.1 | async-start | bytes 524288 | tf_op jit(solution)/shard_map/all_to_all | solution.py:150
Sparse Core Ops, SparseCore 0:
  244.1 66.8 all-gather.2
